TPU v7x, 32 devices: a whole 2x2x4 slice. The times are simulated.
32 devices in a mesh: dp: 4 (over y, x), section: 2 (over core), ctx: 4 (over z).
Axes of the slice: x: 2, y: 2, z: 4, core: 2. Of those that a mesh axis runs over, the one named last changes fastest.
Arguments:
- queries: bfloat16 [4, 2, 512, 2048], P('dp', 'section', 'ctx'), may hold values from -6 to 6
- key_rows: bfloat16 [4, 2, 512, 128], P('dp', 'section', 'ctx'), may hold values from -6 to 6
- value_rows: bfloat16 [4, 2, 512, 128], P('dp', 'section', 'ctx'), may hold values from -6 to 6
- out_grad: bfloat16 [4, 2, 512, 2048], P('dp', 'section', 'ctx'), may hold values from -6 to 6
- attn_out: bfloat16 [4, 2, 512, 2048], P('dp', 'section', 'ctx'), may hold values from -1.796875 to 1.796875
- log_norm: float32 [4, 2, 512, 16], P('dp', 'section', 'ctx'), may hold values from 2 to 5
- selected: int32 [4, 2, 8, 16], P('dp', 'section', 'ctx'), may hold values from -1 to 7, as said below
- gate_weight: float32 [2, 16, 128], P('section'), may hold values from -0.5 to 0.5
- gate_bias: float32 [2, 16], P('section'), may hold values from -2 to 2
Outputs:
- query_grad_prev: bfloat16 [4, 2, 512, 2048], P('dp', 'section', 'ctx')
- key_grad_prev: bfloat16 [4, 2, 512, 128], P('dp', 'section', 'ctx')
- value_grad_prev: bfloat16 [4, 2, 512, 128], P('dp', 'section', 'ctx')
- gate_weight_grad: float32 [2, 16, 128], P('section')
- gate_bias_grad: float32 [2, 16], P('section')
Inputs may be any that keep to these rules, and one draw needn't show every extreme that they name: `selected`: each row of block b lists distinct blocks of 0 to b, always b itself and block 0, min(16, b + 1) of them, followed by -1 entries.
All inputs are finite; a program needn't handle non-finite values.
Results may differ from a plain program's by a relative error of at most 0.013.
Values may be sent and summed in bfloat16 or wider, within the bound.
No kernel may reach another device: no remote copies, remote signals or barrier semaphores. Data moves between devices by JAX's collectives and lax.ppermute only.
A program may use at most 64 MiB of HBM per device.

v0:
```python
import jax
import jax.numpy as jnp
from jax import lax
from jax.sharding import PartitionSpec as P

BLK = 64
SEL = 16


def from_behind(block, axis, distance):
    devices = range(lax.axis_size(axis))
    route = [(i - distance, i) for i in devices if i - distance in devices]
    return lax.ppermute(block, axis, route)


def block_grads(query_blk, grad_blk, delta_blk, norm_blk, allowed, key_part, value_part, factor):
    scores = jnp.dot(query_blk, key_part.T, preferred_element_type=jnp.float32) * factor
    probs = jnp.where(allowed, jnp.exp(jnp.where(allowed, scores - norm_blk[:, None], 0.0)), 0.0)
    probs_b = probs.astype(jnp.bfloat16)
    dprobs = jnp.dot(grad_blk, value_part.T, preferred_element_type=jnp.float32)
    dscores = (probs * (dprobs - delta_blk[:, None])).astype(jnp.bfloat16)
    query_part = factor * jnp.dot(dscores, key_part, preferred_element_type=jnp.float32)
    key_part_grad = factor * jnp.dot(dscores.T, query_blk, preferred_element_type=jnp.float32)
    value_part_grad = jnp.dot(probs_b.T, grad_blk, preferred_element_type=jnp.float32)
    return (query_part, key_part_grad, value_part_grad)


def on_device(
    queries, key_rows, value_rows, out_grad, attn_out, log_norm, selected, gate_weight, gate_bias
):
    query_mat = queries[0, 0]
    length_dev = query_mat.shape[0]
    head_count = gate_weight.shape[1]
    head_dim = gate_weight.shape[2]
    local_blocks = length_dev // BLK
    chosen = selected[0, 0]
    own_keys = key_rows[0, 0]
    own_values = value_rows[0, 0]
    weight = gate_weight[0]
    factor = head_dim ** (-0.5)
    rank_ctx = lax.axis_index("ctx")
    seq_len = length_dev * lax.axis_size("ctx")
    nblocks = seq_len // BLK
    query3 = query_mat.reshape(length_dev, head_count, head_dim).astype(jnp.float32)
    gate = jax.nn.sigmoid(jnp.sum(query3 * weight[None], axis=-1) + gate_bias[0][None])
    grad3 = out_grad[0, 0].reshape(length_dev, head_count, head_dim).astype(jnp.float32)
    output3 = attn_out[0, 0].reshape(length_dev, head_count, head_dim).astype(jnp.float32)
    branch_grad = (gate[:, :, None] * grad3).astype(jnp.bfloat16)
    row_delta = jnp.sum(branch_grad.astype(jnp.float32) * output3, axis=-1)
    pre_grad = jnp.sum(grad3 * output3, axis=-1) * gate * (1.0 - gate)
    rows_total = length_dev * head_count
    query_flat = query_mat.reshape(rows_total, head_dim)
    grad_flat = branch_grad.reshape(rows_total, head_dim)
    delta_flat = row_delta.reshape(-1)
    norm_flat = log_norm[0, 0].reshape(-1)
    query_pos = rank_ctx * length_dev + jnp.arange(rows_total, dtype=jnp.int32) // head_count
    gate_term = (pre_grad[:, :, None] * weight[None]).reshape(rows_total, head_dim)
    key_all, value_all = (
        lax.all_gather(own_keys, "ctx", axis=0, tiled=True),
        lax.all_gather(own_values, "ctx", axis=0, tiled=True),
    )
    safe_ids = jnp.maximum(chosen, 0)
    key_slots = key_all.reshape(nblocks, BLK, head_dim)[safe_ids].reshape(
        local_blocks, SEL * BLK, head_dim
    )
    value_slots = value_all.reshape(nblocks, BLK, head_dim)[safe_ids].reshape(
        local_blocks, SEL * BLK, head_dim
    )
    block_rows = BLK * head_count

    def one_block(items):
        query_blk, grad_blk, delta_blk, norm_blk, pos_blk, chosen_row, key_part, value_part = items
        key_pos = (
            jnp.maximum(chosen_row, 0)[:, None] * BLK + jnp.arange(BLK, dtype=jnp.int32)[None, :]
        ).reshape(-1)
        usable = jnp.repeat(chosen_row >= 0, BLK)
        allowed = usable[None, :] & (key_pos[None, :] <= pos_blk[:, None])
        return block_grads(
            query_blk, grad_blk, delta_blk, norm_blk, allowed, key_part, value_part, factor
        )

    items = (
        query_flat.reshape(local_blocks, block_rows, head_dim),
        grad_flat.reshape(local_blocks, block_rows, head_dim),
        delta_flat.reshape(local_blocks, block_rows),
        norm_flat.reshape(local_blocks, block_rows),
        query_pos.reshape(local_blocks, block_rows),
        chosen,
        key_slots,
        value_slots,
    )
    query_blocks, key_slot_grad, value_slot_grad = lax.map(one_block, items)
    query_acc = query_blocks.reshape(rows_total, head_dim)
    slot_count = local_blocks * SEL
    both_slots = jnp.concatenate(
        [
            key_slot_grad.reshape(slot_count, BLK, head_dim),
            value_slot_grad.reshape(slot_count, BLK, head_dim),
        ],
        axis=-1,
    ).reshape(slot_count, BLK * 2 * head_dim)
    flat_ids = chosen.reshape(-1)
    block_ids = jnp.arange(seq_len // BLK, dtype=jnp.int32)
    one_hot = (flat_ids[None, :] == block_ids[:, None]).astype(jnp.float32)
    placed = jnp.dot(
        one_hot, both_slots, precision=lax.Precision.HIGHEST, preferred_element_type=jnp.float32
    )
    both_full = placed.reshape(seq_len, 2 * head_dim)
    both_mine = lax.psum_scatter(both_full, "ctx", scatter_dimension=0, tiled=True)
    key_mine = both_mine[:, :head_dim]
    value_mine = both_mine[:, head_dim:]
    query_grad = (
        (query_acc + gate_term).astype(jnp.bfloat16).reshape(length_dev, head_count * head_dim)
    )
    query_sent, key_sent, value_sent = from_behind(
        (query_grad, key_mine.astype(jnp.bfloat16), value_mine.astype(jnp.bfloat16)), "section", -1
    )
    weight_local = jnp.sum(pre_grad[:, :, None] * query3, axis=0)
    bias_local = jnp.sum(pre_grad, axis=0)
    weight_total, bias_total = lax.psum((weight_local, bias_local), ("dp", "ctx"))
    return (
        query_sent[None, None],
        key_sent[None, None],
        value_sent[None, None],
        weight_total[None],
        bias_total[None],
    )


def solution(mesh):
    return jax.shard_map(
        on_device,
        mesh=mesh,
        in_specs=(
            P("dp", "section", "ctx", None),
            P("dp", "section", "ctx", None),
            P("dp", "section", "ctx", None),
            P("dp", "section", "ctx", None),
            P("dp", "section", "ctx", None),
            P("dp", "section", "ctx", None),
            P("dp", "section", "ctx", None),
            P("section", None, None),
            P("section", None),
        ),
        out_specs=(
            P("dp", "section", "ctx", None),
            P("dp", "section", "ctx", None),
            P("dp", "section", "ctx", None),
            P("section", None, None),
            P("section", None),
        ),
        check_vma=False,
    )
```

profile of v0, /device:TPU:0, one launch (start us, length us, event | category | flops | bytes accessed | tf_op | source)
XLA Modules:
  0.0 151.8 jit_solution(7226072562469080117)
XLA Ops:
  7.2 0.8 eq.15
  8.0 0.7 broadcast_maximum_fusion
  8.7 2.2 %convert_bitcast_fusion.2 = f32[16,8,16,128]{3,1,2,0:T(8,128)} fusion(bf16[1,1,128,2048]{3,2,1,0:T(8,128)(2,1)} %param.14), kind=kLoop, calls=%fused_computation.56 | loop fusion | flops 262144 | bytes 1572864
  10.9 1.3 reshape.184
  12.2 1.3 reshape_reshape_squeeze.6
  13.5 0.1 convert_bitcast_fusion
  13.6 0.2 copy.25
  13.8 0.3 multiply_reduce_fusion.2
  14.2 0.1 reduce_sum.50
  14.4 0.1 reshape.189
  14.5 0.1 copy.20
  14.6 0.1 reshape_reshape_squeeze.7
  14.7 0.1 add.89
  14.8 15.1 %all-gather = bf16[1,1,512,128]{3,2,1,0:T(8,128)(2,1)S(1)} all-gather(bf16[1,1,128,128]{3,2,1,0:T(8,128)(2,1)S(1)} %copy-done.10), channel_id=2, replica_groups=mesh['dp'=4,'section'=2,'ctx'=4] {'ctx'}, dimensions={2}, use_global_device_ids=true | all-gather | bytes 163840 | tf_op jit(solution)/shard_map/all_gather | solution.py:59
  29.9 13.5 %all-gather.1 = bf16[1,1,512,128]{3,2,1,0:T(8,128)(2,1)S(1)} all-gather(bf16[1,1,128,128]{3,2,1,0:T(8,128)(2,1)S(1)} %copy-done.11), channel_id=3, replica_groups=mesh['dp'=4,'section'=2,'ctx'=4] {'ctx'}, dimensions={2}, use_global_device_ids=true | all-gather | bytes 163840 | tf_op jit(solution)/shard_map/all_gather | solution.py:60
  43.4 1.4 gather_fusion.1
  44.8 0.6 gather_fusion
  45.5 0.1 convert_bitcast_fusion.1
  45.6 1.2 copy.27
  46.8 1.2 copy.26
  47.9 0.1 add_divide_fusion
  48.0 0.1 copy.22
  48.1 2.5 %multiply_reduce_fusion = (f32[128,16]{1,0:T(8,128)S(1)}, f32[128,16]{1,0:T(8,128)S(1)}) fusion(f32[128,16,128]{2,1,0:T(8,128)} %bitcast.126, f32[128,16,128]{2,1,0:T(8,128)} %bitcast.125, f32[128,16]{1,0:T(8,128)S(1)} %copy.22), kind=kLoop, calls=%fused_computation.51 | loop fusion | flops 1830912 | bytes 2121728 | tf_op jit(solution)/shard_map/reduce_sum | solution.py:50
  50.6 0.1 reshape_reshape.4
  50.7 0.3 multiply_convert_fusion.2
  51.0 18.5 %while.14 = (s32[]{:T(128)}, f32[2,1024,128]{2,1,0:T(8,128)}, f32[2,1024,128]{2,1,0:T(8,128)}, f32[2,1024,128]{2,1,0:T(8,128)}, s32[2,16]{1,0:T(2,128)S(1)}, /*i...) while((s32[]{:T(128)}, f32[2,1024,128]{2,1,0:T(8,128)}, ...), condition=%wide.region_3.4_spmd, body=%wide.region_2.0_spmd.sunk | while | flops 1359217664 | bytes 41232960 | solution.py:92
  51.2 0.1 and.48
  51.4 0.7 fusion.70
  52.2 2.6 %fusion.73 = f32[2,1024,128]{2,1,0:T(8,128)} fusion(f32[2,1024,128]{2,1,0:T(8,128)} %get-tuple-element.199, s32[]{:T(128)S(6)} %copy.38, f32[1024,1024]{1,0:T(8,128)S(1)} %fusion.70, f32[1024]{0:T(1024)S(1)} %bitcast.135, s32[1024]{0:T(1024)S(1)} %add.124, s32[1024]{0:T(1024)S(1)} %bitcast.132, pred[1024]{0:T(1024)(128)(4,1)S(1)} %and.48, ...), kind=kOutput, calls=%fused_computation.7.clone.1 | convolution fusion | flops 275775488 | bytes 4995072 | tf_op jit(solution)/shard_map/while/body/eval_jaxpr/dot_general | solution.py:24
  54.8 2.2 %multiply_convert_fusion.4 = bf16[1024,1024]{1,0:T(8,128)(2,1)S(1)} fusion(f32[1024,1024]{1,0:T(8,128)S(1)} %fusion.70, f32[1024]{0:T(1024)S(1)} %bitcast.134, f32[1024]{0:T(1024)S(1)} %bitcast.136, s32[1024]{0:T(1024)S(1)} %add.124, s32[1024]{0:T(1024)S(1)} %bitcast.133, pred[1024]{0:T(1024)(128)(4,1)S(1)} %and.48, ...), kind=kOutput, calls=%fused_computation.2.clone.1 | convolution fusion | flops 277872640 | bytes 6834176 | tf_op jit(solution)/shard_map/while/body/eval_jaxpr/dot_general | solution.py:20
  57.1 0.8 fusion.72
  57.8 0.4 copy-done.2
  58.3 0.7 fusion.71
  59.0 0.3 copy-done.6
  59.3 1.0 copy-done.3
  60.4 0.1 and.48
  60.6 0.7 fusion.70
  61.4 2.6 %fusion.73 = f32[2,1024,128]{2,1,0:T(8,128)} fusion(f32[2,1024,128]{2,1,0:T(8,128)} %get-tuple-element.199, s32[]{:T(128)S(6)} %copy.38, f32[1024,1024]{1,0:T(8,128)S(1)} %fusion.70, f32[1024]{0:T(1024)S(1)} %bitcast.135, s32[1024]{0:T(1024)S(1)} %add.124, s32[1024]{0:T(1024)S(1)} %bitcast.132, pred[1024]{0:T(1024)(128)(4,1)S(1)} %and.48, ...), kind=kOutput, calls=%fused_computation.7.clone.1 | convolution fusion | flops 275775488 | bytes 4995072 | tf_op jit(solution)/shard_map/while/body/eval_jaxpr/dot_general | solution.py:24
  64.0 2.3 %multiply_convert_fusion.4 = bf16[1024,1024]{1,0:T(8,128)(2,1)S(1)} fusion(f32[1024,1024]{1,0:T(8,128)S(1)} %fusion.70, f32[1024]{0:T(1024)S(1)} %bitcast.134, f32[1024]{0:T(1024)S(1)} %bitcast.136, s32[1024]{0:T(1024)S(1)} %add.124, s32[1024]{0:T(1024)S(1)} %bitcast.133, pred[1024]{0:T(1024)(128)(4,1)S(1)} %and.48, ...), kind=kOutput, calls=%fused_computation.2.clone.1 | convolution fusion | flops 277872640 | bytes 6834176 | tf_op jit(solution)/shard_map/while/body/eval_jaxpr/dot_general | solution.py:20
  66.3 0.8 fusion.72
  67.0 0.4 copy-done.2
  67.5 0.7 fusion.71
  68.2 0.3 copy-done.6
  68.5 1.0 copy-done.3
  69.5 1.7 %pad_maximum_fusion = f32[32,64,256]{2,1,0:T(8,128)S(1)} fusion(f32[32,64,128]{2,1,0:T(8,128)} %bitcast.22, f32[32,64,128]{2,1,0:T(8,128)} %bitcast.130), kind=kLoop, calls=%fused_computation.43 | loop fusion | flops 524288 | bytes 4194304 | tf_op jit(solution)/shard_map/concatenate | solution.py:95
  71.2 1.2 copy.29
  72.4 0.8 fusion.39
  73.3 0.9 reshape.181
  74.2 0.2 fusion.41
  74.4 0.1 copy.24
  74.5 0.2 reshape.177
  74.7 0.3 mul.125
  75.0 0.5 fusion.37
  75.5 1.3 collective-permute-start
  76.8 0.2 mul.130
  77.0 20.3 %reduce-scatter.2.cloned.1.call-done = f32[128,256]{1,0:T(8,128)} async-done(((f32[512,256]{1,0:T(8,128)}), f32[128,256]{1,0:T(8,128)}) %reduce-scatter.2.cloned.1.call-update) | async-done | bytes 131088 | tf_op jit(solution)/shard_map/reduce_scatter | solution.py:109
  97.3 0.9 convert.8
  98.2 1.3 collective-permute-start.2
  99.5 1.3 collective-permute-start.1
  100.8 0.1 fusion.35
  100.9 40.9 %all-reduce = (f32[1,16,128]{2,1,0:T(8,128)}, f32[1,16]{1,0:T(1,128)}) all-reduce(f32[1,16,128]{2,1,0:T(8,128)S(1)} %bitcast.139, f32[1,16]{1,0:T(1,128)S(1)} %bitcast.145), channel_id=1, replica_groups=mesh['dp'=4,'section'=2,'ctx'=4] {'dp','ctx'}, use_global_device_ids=true, to_apply=%region_7.8 | all-reduce | flops 2064 | bytes 16512 | tf_op jit(solution)/shard_map/psum | solution.py:120
  141.8 1.9 %copy.51 = bf16[1,1,128,2048]{3,2,1,0:T(8,128)(2,1)} copy(bf16[1,1,128,2048]{3,2,1,0:T(8,128)(2,1)} %bitcast.20) | data formatting | bytes 1048576
  143.7 0.6 copy.52
  144.3 0.6 copy.53
  (63 shorter events, 0.8 us)
Async XLA Ops:
  7.2 6.3 %copy-start = (bf16[1,1,128,2048]{3,2,1,0:T(8,128)(2,1)S(1)}, bf16[1,1,128,2048]{3,2,1,0:T(8,128)(2,1)}, u32[]{:S(2)}) copy-start(bf16[1,1,128,2048]{3,2,1,0:T(8,128)(2,1)} %param.11) | copy-start | bytes 1572868
  7.2 6.7 %copy-start.9 = (f32[1,16,128]{2,1,0:T(8,128)S(1)}, f32[1,16,128]{2,1,0:T(8,128)}, u32[]{:S(2)}) copy-start(f32[1,16,128]{2,1,0:T(8,128)} %param.18) | copy-start | bytes 24580
  7.2 90.1 %reduce-scatter.2.cloned.1.call-start = ((), (), s32[]{:S(2)}) async-start(), calls=%async_computation.1 | async-start | bytes 655360 | tf_op jit(solution)/shard_map/reduce_scatter | solution.py:109
  8.7 5.8 %copy-start.12 = (f32[1,1,128,16]{2,3,1,0:T(8,128)S(1)}, f32[1,1,128,16]{2,3,1,0:T(8,128)}, u32[]{:S(2)}) copy-start(f32[1,1,128,16]{2,3,1,0:T(8,128)} %param.16) | copy-start | bytes 24580
  10.9 3.8 %copy-start.13 = (f32[1,16]{1,0:T(1,128)S(1)}, f32[1,16]{1,0:T(1,128)}, u32[]{:S(2)}) copy-start(f32[1,16]{1,0:T(1,128)} %param.19) | copy-start | bytes 196
  10.9 4.0 %copy-start.10 = (bf16[1,1,128,128]{3,2,1,0:T(8,128)(2,1)S(1)}, bf16[1,1,128,128]{3,2,1,0:T(8,128)(2,1)}, u32[]{:S(2)}) copy-start(bf16[1,1,128,128]{3,2,1,0:T(8,128)(2,1)} %param.12) | copy-start | bytes 98308
  10.9 19.0 %copy-start.11 = (bf16[1,1,128,128]{3,2,1,0:T(8,128)(2,1)S(1)}, bf16[1,1,128,128]{3,2,1,0:T(8,128)(2,1)}, u32[]{:S(2)}) copy-start(bf16[1,1,128,128]{3,2,1,0:T(8,128)(2,1)} %param.13) | copy-start | bytes 98308
  12.2 33.3 %copy-start.7 = (bf16[1,1,128,2048]{3,2,1,0:T(8,128)(2,1)S(1)}, bf16[1,1,128,2048]{3,2,1,0:T(8,128)(2,1)}, u32[]{:S(2)}) copy-start(bf16[1,1,128,2048]{3,2,1,0:T(8,128)(2,1)} %param.15) | copy-start | bytes 1572868
  45.5 1.3 copy-start.1
  45.6 5.5 %copy-start.14 = (s32[1,1,2,16]{3,2,1,0:T(2,128)S(1)}, s32[1,1,2,16]{3,2,1,0:T(2,128)}, u32[]{:S(2)}) copy-start(s32[1,1,2,16]{3,2,1,0:T(2,128)} %param.17) | copy-start | bytes 388
  52.1 2.6 %copy-start.8 = (bf16[2,1024,128]{2,1,0:T(8,128)(2,1)S(1)}, bf16[2,1024,128]{2,1,0:T(8,128)(2,1)}, u32[]{:S(2)}) copy-start(bf16[2,1024,128]{2,1,0:T(8,128)(2,1)} %get-tuple-element.219) | copy-start | bytes 1572868 | tf_op jit(solution)/shard_map/while
  54.8 2.3 %copy-start.5 = (f32[2,1024,128]{2,1,0:T(8,128)S(1)}, f32[2,1024,128]{2,1,0:T(8,128)}, u32[]{:S(2)}) copy-start(f32[2,1024,128]{2,1,0:T(8,128)} %get-tuple-element.198) | copy-start | bytes 3145732 | tf_op jit(solution)/shard_map/while
  57.0 1.2 copy-start.2
  58.3 1.0 copy-start.6
  59.3 1.0 copy-start.3
  61.4 2.6 %copy-start.8 = (bf16[2,1024,128]{2,1,0:T(8,128)(2,1)S(1)}, bf16[2,1024,128]{2,1,0:T(8,128)(2,1)}, u32[]{:S(2)}) copy-start(bf16[2,1024,128]{2,1,0:T(8,128)(2,1)} %get-tuple-element.219) | copy-start | bytes 1572868 | tf_op jit(solution)/shard_map/while
  64.0 2.3 %copy-start.5 = (f32[2,1024,128]{2,1,0:T(8,128)S(1)}, f32[2,1024,128]{2,1,0:T(8,128)}, u32[]{:S(2)}) copy-start(f32[2,1024,128]{2,1,0:T(8,128)} %get-tuple-element.198) | copy-start | bytes 3145732 | tf_op jit(solution)/shard_map/while
  66.3 1.2 copy-start.2
  67.5 1.0 copy-start.6
  68.5 1.0 copy-start.3
  71.2 3.3 %copy-start.4 = (f32[2,1024,128]{2,1,0:T(8,128)S(1)}, f32[2,1024,128]{2,1,0:T(8,128)}, u32[]{:S(2)}) copy-start(f32[2,1024,128]{2,1,0:T(8,128)} %get-tuple-element.69) | copy-start | bytes 3145732
  75.5 66.3 %collective-permute-start = (bf16[128,2048]{1,0:T(8,128)(2,1)S(1)}, bf16[128,2048]{1,0:T(8,128)(2,1)}, u32[]{:S(2)}, u32[]{:S(2)}) collective-permute-start(bf16[128,2048]{1,0:T(8,128)(2,1)S(1)} %fusion.37), channel_id=1, source_target_pairs={{4,0},{5,1},{6,2},{7,3},{12,8},{13,9},{14,10},{15,11},{20,16},{21,... | collective-permute-start | bytes 1572872 | tf_op jit(solution)/shard_map/ppermute | solution.py:13
  98.2 43.6 %collective-permute-start.2 = (bf16[128,128]{1,0:T(8,128)(2,1)S(1)}, bf16[128,128]{1,0:T(8,128)(2,1)S(1)}, u32[]{:S(2)}, u32[]{:S(2)}) collective-permute-start(bf16[128,128]{1,0:T(8,128)(2,1)S(1)} %get-tuple-element.104), channel_id=1, source_target_pairs={{4,0},{5,1},{6,2},{7,3},{12,8},{13,9},{14,10},{15,11},{20,16},{21,... | collective-permute-start | bytes 98312 | tf_op jit(solution)/shard_map/ppermute | solution.py:13
  99.5 42.3 %collective-permute-start.1 = (bf16[128,128]{1,0:T(8,128)(2,1)S(1)}, bf16[128,128]{1,0:T(8,128)(2,1)S(1)}, u32[]{:S(2)}, u32[]{:S(2)}) collective-permute-start(bf16[128,128]{1,0:T(8,128)(2,1)S(1)} %get-tuple-element.105), channel_id=1, source_target_pairs={{4,0},{5,1},{6,2},{7,3},{12,8},{13,9},{14,10},{15,11},{20,16},{21,... | collective-permute-start | bytes 98312 | tf_op jit(solution)/shard_map/ppermute | solution.py:13
Sparse Core Ops, SparseCore 0:
  74.3 22.9 reduce-scatter.1
where the time goes:
time: 152 us
  blocking collectives  69.4 us (46%)
  waiting for transfers between devices  20.3 us (13%)
  local copies, waits for them, and re-layouts  18.8 us (12%)
  matrix products  14.9 us (10%)
  between operations  14.4 us (9%)
  other arithmetic  9.91 us (7%)
  starting transfers between devices  3.91 us (3%)
    psum x1, blocking collectives, on_device(): lax.psum((weight_local, bias_local), ('dp', 'ctx'))  40.9 us
    reduce_scatter x1, waiting for transfers between devices, on_device(): lax.psum_scatter(both_full, 'ctx', scatter_dimension=0, tiled=True)  20.3 us
    all_gather x1, blocking collectives, on_device(): lax.all_gather(own_keys, 'ctx', axis=0, tiled=True)  15.1 us
    all_gather x1, blocking collectives, on_device(): lax.all_gather(own_values, 'ctx', axis=0, tiled=True)  13.5 us
    unnamed x28, local copies, waits for them, and re-layouts  7 us
    dot_general x2, matrix products, block_grads(): jnp.dot(probs_b.T, grad_blk, preferred_element_type=jnp.float32)  5.24 us
    dot_general x2, matrix products, block_grads(): dprobs = jnp.dot(grad_blk, value_part.T, preferred_element_type=jnp.float32)  4.5 us
    ppermute x3, starting transfers between devices, from_behind(): return lax.ppermute(block, axis, route)  3.88 us
  transfers between devices with their start and end apart: 4, of which 1 were waited for; matrix products, arithmetic and copies ran while one was open for 2% of the time, Pallas kernels for 0%

commit v1 on v0

--- a/solution.py
+++ b/solution.py
@@ -117,7 +117,7 @@
     )
     weight_local = jnp.sum(pre_grad[:, :, None] * query3, axis=0)
     bias_local = jnp.sum(pre_grad, axis=0)
-    weight_total, bias_total = lax.psum((weight_local, bias_local), ("dp", "ctx"))
+    weight_total, bias_total = lax.psum(lax.psum((weight_local, bias_local), "ctx"), "dp")
     return (
         query_sent[None, None],
         key_sent[None, None],

time: 152 us -> 131 us (0.86)
  blocking collectives: 69.4 us -> 48.5 us
    psum x1 -> x2, blocking collectives: 40.9 us -> 19.9 us  [the longest x1 10.8 us: on_device(): lax.psum(lax.psum((weight_local, bias_local), 'ctx'), 'dp')]
where the time goes in v1:
time: 131 us
  blocking collectives  48.5 us (37%)
  waiting for transfers between devices  20.3 us (15%)
  local copies, waits for them, and re-layouts  18.7 us (14%)
  matrix products  14.9 us (11%)
  between operations  14.4 us (11%)
  other arithmetic  9.9 us (8%)
  starting transfers between devices  3.91 us (3%)
    reduce_scatter x1, waiting for transfers between devices, on_device(): lax.psum_scatter(both_full, 'ctx', scatter_dimension=0, tiled=True)  20.3 us
    all_gather x1, blocking collectives, on_device(): lax.all_gather(own_keys, 'ctx', axis=0, tiled=True)  15.1 us
    all_gather x1, blocking collectives, on_device(): lax.all_gather(own_values, 'ctx', axis=0, tiled=True)  13.5 us
    psum x1, blocking collectives, on_device(): lax.psum(lax.psum((weight_local, bias_local), 'ctx'), 'dp')  10.8 us
    psum x1, blocking collectives, on_device(): lax.psum((weight_local, bias_local), 'ctx')  9.16 us
    unnamed x28, local copies, waits for them, and re-layouts  7 us
    dot_general x2, matrix products, block_grads(): jnp.dot(probs_b.T, grad_blk, preferred_element_type=jnp.float32)  5.23 us
    dot_general x2, matrix products, block_grads(): dprobs = jnp.dot(grad_blk, value_part.T, preferred_element_type=jnp.float32)  4.5 us
  transfers between devices with their start and end apart: 4, of which 1 were waited for; matrix products, arithmetic and copies ran while one was open for 2% of the time, Pallas kernels for 0%

profile of v1, /device:TPU:0, one launch (start us, length us, event | category | flops | bytes accessed | tf_op | source)
XLA Modules:
  0.0 130.7 jit_solution(17942588480993108256)
XLA Ops:
  7.2 0.8 eq.15
  8.0 0.7 broadcast_maximum_fusion
  8.7 2.1 %convert_bitcast_fusion.2 = f32[16,8,16,128]{3,1,2,0:T(8,128)} fusion(bf16[1,1,128,2048]{3,2,1,0:T(8,128)(2,1)} %param.14), kind=kLoop, calls=%fused_computation.56 | loop fusion | flops 262144 | bytes 1572864
  10.9 1.3 reshape.183
  12.2 1.3 %reshape_reshape_squeeze.6 = bf16[2,1024,128]{2,1,0:T(8,128)(2,1)S(1)} reshape(bf16[1,1,128,2048]{3,2,1,0:T(8,128)(2,1)} %param.11) | data formatting | bytes 1048576 | tf_op jit(solution)/shard_map/reshape;reshape;squeeze | solution.py:83
  13.5 0.1 convert_bitcast_fusion
  13.6 0.2 copy.25
  13.8 0.3 multiply_reduce_fusion.2
  14.2 0.1 reduce_sum.50
  14.4 0.1 reshape.188
  14.5 0.1 copy.20
  14.6 0.1 reshape_reshape_squeeze.7
  14.7 0.1 add.93
  14.8 15.1 %all-gather = bf16[1,1,512,128]{3,2,1,0:T(8,128)(2,1)S(1)} all-gather(bf16[1,1,128,128]{3,2,1,0:T(8,128)(2,1)S(1)} %copy-done.10), channel_id=2, replica_groups=mesh['dp'=4,'section'=2,'ctx'=4] {'ctx'}, dimensions={2}, use_global_device_ids=true | all-gather | bytes 163840 | tf_op jit(solution)/shard_map/all_gather | solution.py:59
  29.9 13.5 %all-gather.1 = bf16[1,1,512,128]{3,2,1,0:T(8,128)(2,1)S(1)} all-gather(bf16[1,1,128,128]{3,2,1,0:T(8,128)(2,1)S(1)} %copy-done.11), channel_id=3, replica_groups=mesh['dp'=4,'section'=2,'ctx'=4] {'ctx'}, dimensions={2}, use_global_device_ids=true | all-gather | bytes 163840 | tf_op jit(solution)/shard_map/all_gather | solution.py:60
  43.4 1.4 %gather_fusion.1 = bf16[32,64,128]{2,1,0:T(8,128)(2,1)} fusion(bf16[8,64,128]{2,1,0:T(8,128)(2,1)S(1)} %bitcast.130, s32[1024]{0:T(1024)S(1)} %pad_clamp_fusion), kind=kCustom, calls=%fused_computation.1 | custom fusion | bytes 1048704 | tf_op jit(solution)/shard_map/gather | solution.py:66
  44.8 0.6 gather_fusion
  45.5 0.1 convert_bitcast_fusion.1
  45.6 1.2 copy.27
  46.8 1.2 copy.26
  48.0 0.1 copy.22
  48.1 2.5 %multiply_reduce_fusion = (f32[128,16]{1,0:T(8,128)S(1)}, f32[128,16]{1,0:T(8,128)S(1)}) fusion(f32[128,16,128]{2,1,0:T(8,128)} %bitcast.127, f32[128,16,128]{2,1,0:T(8,128)} %bitcast.126, f32[128,16]{1,0:T(8,128)S(1)} %copy.22), kind=kLoop, calls=%fused_computation.51 | loop fusion | flops 1830912 | bytes 2121728 | tf_op jit(solution)/shard_map/reduce_sum | solution.py:50
  50.6 0.1 reshape_reshape.4
  50.7 0.3 multiply_convert_fusion.2
  51.0 18.4 %while.14 = (s32[]{:T(128)}, f32[2,1024,128]{2,1,0:T(8,128)}, f32[2,1024,128]{2,1,0:T(8,128)}, f32[2,1024,128]{2,1,0:T(8,128)}, s32[2,16]{1,0:T(2,128)S(1)}, /*i...) while((s32[]{:T(128)}, f32[2,1024,128]{2,1,0:T(8,128)}, ...), condition=%wide.region_3.4_spmd, body=%wide.region_2.0_spmd.sunk | while | flops 1359217664 | bytes 41232960 | solution.py:92
  51.2 0.1 and.48
  51.4 0.7 fusion.70
  52.1 2.6 %fusion.73 = f32[2,1024,128]{2,1,0:T(8,128)} fusion(f32[2,1024,128]{2,1,0:T(8,128)} %get-tuple-element.201, s32[]{:T(128)S(6)} %copy.38, f32[1024,1024]{1,0:T(8,128)S(1)} %fusion.70, f32[1024]{0:T(1024)S(1)} %bitcast.136, s32[1024]{0:T(1024)S(1)} %add.128, s32[1024]{0:T(1024)S(1)} %bitcast.133, pred[1024]{0:T(1024)(128)(4,1)S(1)} %and.48, ...), kind=kOutput, calls=%fused_computation.7.clone.1 | convolution fusion | flops 275775488 | bytes 4995072 | tf_op jit(solution)/shard_map/while/body/eval_jaxpr/dot_general | solution.py:24
  54.8 2.3 %multiply_convert_fusion.4 = bf16[1024,1024]{1,0:T(8,128)(2,1)S(1)} fusion(f32[1024,1024]{1,0:T(8,128)S(1)} %fusion.70, f32[1024]{0:T(1024)S(1)} %bitcast.135, f32[1024]{0:T(1024)S(1)} %bitcast.137, s32[1024]{0:T(1024)S(1)} %add.128, s32[1024]{0:T(1024)S(1)} %bitcast.134, pred[1024]{0:T(1024)(128)(4,1)S(1)} %and.48, ...), kind=kOutput, calls=%fused_computation.2.clone.1 | convolution fusion | flops 277872640 | bytes 6834176 | tf_op jit(solution)/shard_map/while/body/eval_jaxpr/dot_general | solution.py:20
  57.0 0.8 fusion.72
  57.8 0.4 copy-done.2
  58.3 0.7 fusion.71
  59.0 0.3 copy-done.6
  59.3 1.0 copy-done.3
  60.3 0.1 and.48
  60.6 0.7 fusion.70
  61.3 2.6 %fusion.73 = f32[2,1024,128]{2,1,0:T(8,128)} fusion(f32[2,1024,128]{2,1,0:T(8,128)} %get-tuple-element.201, s32[]{:T(128)S(6)} %copy.38, f32[1024,1024]{1,0:T(8,128)S(1)} %fusion.70, f32[1024]{0:T(1024)S(1)} %bitcast.136, s32[1024]{0:T(1024)S(1)} %add.128, s32[1024]{0:T(1024)S(1)} %bitcast.133, pred[1024]{0:T(1024)(128)(4,1)S(1)} %and.48, ...), kind=kOutput, calls=%fused_computation.7.clone.1 | convolution fusion | flops 275775488 | bytes 4995072 | tf_op jit(solution)/shard_map/while/body/eval_jaxpr/dot_general | solution.py:24
  63.9 2.3 %multiply_convert_fusion.4 = bf16[1024,1024]{1,0:T(8,128)(2,1)S(1)} fusion(f32[1024,1024]{1,0:T(8,128)S(1)} %fusion.70, f32[1024]{0:T(1024)S(1)} %bitcast.135, f32[1024]{0:T(1024)S(1)} %bitcast.137, s32[1024]{0:T(1024)S(1)} %add.128, s32[1024]{0:T(1024)S(1)} %bitcast.134, pred[1024]{0:T(1024)(128)(4,1)S(1)} %and.48, ...), kind=kOutput, calls=%fused_computation.2.clone.1 | convolution fusion | flops 277872640 | bytes 6834176 | tf_op jit(solution)/shard_map/while/body/eval_jaxpr/dot_general | solution.py:20
  66.2 0.8 fusion.72
  67.0 0.4 copy-done.2
  67.4 0.7 fusion.71
  68.1 0.3 copy-done.6
  68.4 1.0 copy-done.3
  69.4 1.7 %pad_maximum_fusion = f32[32,64,256]{2,1,0:T(8,128)S(1)} fusion(f32[32,64,128]{2,1,0:T(8,128)} %bitcast.22, f32[32,64,128]{2,1,0:T(8,128)} %bitcast.131), kind=kLoop, calls=%fused_computation.43 | loop fusion | flops 524288 | bytes 4194304 | tf_op jit(solution)/shard_map/concatenate | solution.py:95
  71.1 1.2 copy.29
  72.4 0.8 fusion.39
  73.2 0.9 reshape.181
  74.1 0.2 fusion.41
  74.3 0.1 copy.24
  74.5 0.2 reshape.177
  74.6 0.3 mul.125
  75.0 0.5 fusion.37
  75.4 1.3 collective-permute-start
  76.7 0.2 mul.130
  76.9 20.3 %reduce-scatter.2.cloned.1.call-done = f32[128,256]{1,0:T(8,128)} async-done(((f32[512,256]{1,0:T(8,128)}), f32[128,256]{1,0:T(8,128)}) %reduce-scatter.2.cloned.1.call-update) | async-done | bytes 131088 | tf_op jit(solution)/shard_map/reduce_scatter | solution.py:109
  97.2 0.9 convert.8
  98.1 1.3 collective-permute-start.2
  99.4 1.3 collective-permute-start.1
  100.7 0.1 fusion.35
  100.8 9.2 %all-reduce = (f32[16,128]{1,0:T(8,128)S(1)}, f32[16]{0:T(128)S(1)}) all-reduce(f32[16,128]{1,0:T(8,128)S(1)} %bitcast.140, f32[16]{0:T(128)S(1)} %get-tuple-element.102), channel_id=1, replica_groups=mesh['dp'=4,'section'=2,'ctx'=4] {'ctx'}, use_global_device_ids=true, to_apply=%region_7.8 | all-reduce | flops 2064 | bytes 16512 | tf_op jit(solution)/shard_map/psum | solution.py:120
  110.0 10.8 %all-reduce.1 = (f32[1,16,128]{2,1,0:T(8,128)}, f32[1,16]{1,0:T(1,128)}) all-reduce(f32[1,16,128]{2,1,0:T(8,128)S(1)} %bitcast.143, f32[1,16]{1,0:T(1,128)S(1)} %bitcast.148), channel_id=1, replica_groups=mesh['dp'=4,'section'=2,'ctx'=4] {'dp'}, use_global_device_ids=true, to_apply=%region_8.9 | all-reduce | flops 2064 | bytes 16512 | tf_op jit(solution)/shard_map/psum | solution.py:120
  120.8 1.9 %copy.51 = bf16[1,1,128,2048]{3,2,1,0:T(8,128)(2,1)} copy(bf16[1,1,128,2048]{3,2,1,0:T(8,128)(2,1)} %bitcast.20) | data formatting | bytes 1048576
  122.6 0.6 copy.52
  123.3 0.6 copy.53
  (64 shorter events, 0.9 us)
Async XLA Ops:
  7.2 6.3 %copy-start = (bf16[1,1,128,2048]{3,2,1,0:T(8,128)(2,1)S(1)}, bf16[1,1,128,2048]{3,2,1,0:T(8,128)(2,1)}, u32[]{:S(2)}) copy-start(bf16[1,1,128,2048]{3,2,1,0:T(8,128)(2,1)} %param.11) | copy-start | bytes 1572868
  7.2 6.6 %copy-start.9 = (f32[1,16,128]{2,1,0:T(8,128)S(1)}, f32[1,16,128]{2,1,0:T(8,128)}, u32[]{:S(2)}) copy-start(f32[1,16,128]{2,1,0:T(8,128)} %param.18) | copy-start | bytes 24580
  7.2 90.0 %reduce-scatter.2.cloned.1.call-start = ((), (), s32[]{:S(2)}) async-start(), calls=%async_computation.1 | async-start | bytes 655360 | tf_op jit(solution)/shard_map/reduce_scatter | solution.py:109
  8.7 5.8 %copy-start.12 = (f32[1,1,128,16]{2,3,1,0:T(8,128)S(1)}, f32[1,1,128,16]{2,3,1,0:T(8,128)}, u32[]{:S(2)}) copy-start(f32[1,1,128,16]{2,3,1,0:T(8,128)} %param.16) | copy-start | bytes 24580
  10.9 3.8 %copy-start.13 = (f32[1,16]{1,0:T(1,128)S(1)}, f32[1,16]{1,0:T(1,128)}, u32[]{:S(2)}) copy-start(f32[1,16]{1,0:T(1,128)} %param.19) | copy-start | bytes 196
  10.9 4.0 %copy-start.10 = (bf16[1,1,128,128]{3,2,1,0:T(8,128)(2,1)S(1)}, bf16[1,1,128,128]{3,2,1,0:T(8,128)(2,1)}, u32[]{:S(2)}) copy-start(bf16[1,1,128,128]{3,2,1,0:T(8,128)(2,1)} %param.12) | copy-start | bytes 98308
  10.9 19.0 %copy-start.11 = (bf16[1,1,128,128]{3,2,1,0:T(8,128)(2,1)S(1)}, bf16[1,1,128,128]{3,2,1,0:T(8,128)(2,1)}, u32[]{:S(2)}) copy-start(bf16[1,1,128,128]{3,2,1,0:T(8,128)(2,1)} %param.13) | copy-start | bytes 98308
  12.1 33.3 %copy-start.7 = (bf16[1,1,128,2048]{3,2,1,0:T(8,128)(2,1)S(1)}, bf16[1,1,128,2048]{3,2,1,0:T(8,128)(2,1)}, u32[]{:S(2)}) copy-start(bf16[1,1,128,2048]{3,2,1,0:T(8,128)(2,1)} %param.15) | copy-start | bytes 1572868
  45.5 1.3 copy-start.1
  45.6 5.5 %copy-start.14 = (s32[1,1,2,16]{3,2,1,0:T(2,128)S(1)}, s32[1,1,2,16]{3,2,1,0:T(2,128)}, u32[]{:S(2)}) copy-start(s32[1,1,2,16]{3,2,1,0:T(2,128)} %param.17) | copy-start | bytes 388
  52.1 2.6 %copy-start.8 = (bf16[2,1024,128]{2,1,0:T(8,128)(2,1)S(1)}, bf16[2,1024,128]{2,1,0:T(8,128)(2,1)}, u32[]{:S(2)}) copy-start(bf16[2,1024,128]{2,1,0:T(8,128)(2,1)} %get-tuple-element.221) | copy-start | bytes 1572868 | tf_op jit(solution)/shard_map/while
  54.8 2.3 %copy-start.5 = (f32[2,1024,128]{2,1,0:T(8,128)S(1)}, f32[2,1024,128]{2,1,0:T(8,128)}, u32[]{:S(2)}) copy-start(f32[2,1024,128]{2,1,0:T(8,128)} %get-tuple-element.200) | copy-start | bytes 3145732 | tf_op jit(solution)/shard_map/while
  57.0 1.2 copy-start.2
  58.3 1.0 copy-start.6
  59.3 1.0 copy-start.3
  61.3 2.6 %copy-start.8 = (bf16[2,1024,128]{2,1,0:T(8,128)(2,1)S(1)}, bf16[2,1024,128]{2,1,0:T(8,128)(2,1)}, u32[]{:S(2)}) copy-start(bf16[2,1024,128]{2,1,0:T(8,128)(2,1)} %get-tuple-element.221) | copy-start | bytes 1572868 | tf_op jit(solution)/shard_map/while
  63.9 2.3 %copy-start.5 = (f32[2,1024,128]{2,1,0:T(8,128)S(1)}, f32[2,1024,128]{2,1,0:T(8,128)}, u32[]{:S(2)}) copy-start(f32[2,1024,128]{2,1,0:T(8,128)} %get-tuple-element.200) | copy-start | bytes 3145732 | tf_op jit(solution)/shard_map/while
  66.2 1.2 copy-start.2
  67.4 1.0 copy-start.6
  68.4 1.0 copy-start.3
  71.1 3.3 %copy-start.4 = (f32[2,1024,128]{2,1,0:T(8,128)S(1)}, f32[2,1024,128]{2,1,0:T(8,128)}, u32[]{:S(2)}) copy-start(f32[2,1024,128]{2,1,0:T(8,128)} %get-tuple-element.69) | copy-start | bytes 3145732
  75.4 45.3 %collective-permute-start = (bf16[128,2048]{1,0:T(8,128)(2,1)S(1)}, bf16[128,2048]{1,0:T(8,128)(2,1)}, u32[]{:S(2)}, u32[]{:S(2)}) collective-permute-start(bf16[128,2048]{1,0:T(8,128)(2,1)S(1)} %fusion.37), channel_id=1, source_target_pairs={{4,0},{5,1},{6,2},{7,3},{12,8},{13,9},{14,10},{15,11},{20,16},{21,... | collective-permute-start | bytes 1572872 | tf_op jit(solution)/shard_map/ppermute | solution.py:13
  98.1 22.7 %collective-permute-start.2 = (bf16[128,128]{1,0:T(8,128)(2,1)S(1)}, bf16[128,128]{1,0:T(8,128)(2,1)S(1)}, u32[]{:S(2)}, u32[]{:S(2)}) collective-permute-start(bf16[128,128]{1,0:T(8,128)(2,1)S(1)} %get-tuple-element.106), channel_id=1, source_target_pairs={{4,0},{5,1},{6,2},{7,3},{12,8},{13,9},{14,10},{15,11},{20,16},{21,... | collective-permute-start | bytes 98312 | tf_op jit(solution)/shard_map/ppermute | solution.py:13
  99.4 21.4 %collective-permute-start.1 = (bf16[128,128]{1,0:T(8,128)(2,1)S(1)}, bf16[128,128]{1,0:T(8,128)(2,1)S(1)}, u32[]{:S(2)}, u32[]{:S(2)}) collective-permute-start(bf16[128,128]{1,0:T(8,128)(2,1)S(1)} %get-tuple-element.107), channel_id=1, source_target_pairs={{4,0},{5,1},{6,2},{7,3},{12,8},{13,9},{14,10},{15,11},{20,16},{21,... | collective-permute-start | bytes 98312 | tf_op jit(solution)/shard_map/ppermute | solution.py:13
Sparse Core Ops, SparseCore 0:
  74.2 22.9 reduce-scatter.1
